TPU v7x, 256 devices: a whole 4x4x8 slice. The times are simulated.
256 devices in a mesh: seq: 32 (over x_lo, z, core), chan: 8 (over x_hi, y).
Axes of the slice: x: 4 (x_hi: 2, x_lo: 2; x = x_hi * 2 + x_lo), y: 4, z: 8, core: 2. Of those that a mesh axis runs over, the one named last changes fastest.
Arguments:
- inputs: bfloat16 [262144, 1024], P('seq', 'chan'), may hold values from -6 to 6
- out_grad: bfloat16 [262144, 1024], P('seq', 'chan'), may hold values from -6 to 6
- kernel: bfloat16 [512, 512, 1024], P('seq', None, 'chan'), may hold values from -4 to 4
- gate_weight: bfloat16 [1024, 1024], P(None, 'chan'), may hold values from -0.1875 to 0.1875
- right_factor: bfloat16 [512, 512], replicated, may hold values from -0.25 to 0.25
- left_factor: bfloat16 [512, 512], replicated, may hold values from -0.25 to 0.25
Outputs:
- input_grad: bfloat16 [262144, 1024], P('seq', 'chan')
- kernel_grad: bfloat16 [512, 512, 1024], P('seq', None, 'chan')
- right_grad: float32 [262144], P(('seq', 'chan'))
- left_grad: float32 [262144], P(('seq', 'chan'))
- gate_weight_grad: float32 [1024, 1024], P(('seq', 'chan'))
All inputs are finite; a program needn't handle non-finite values.
Results may differ from a plain program's by a relative error of at most 0.015.
Values may be sent and summed in bfloat16 or wider, within the bound.
No kernel may reach another device: no remote copies, remote signals or barrier semaphores. Data moves between devices by JAX's collectives and lax.ppermute only.
A program may use at most 128 MiB of HBM per device.

v0:
```python
import jax
import jax.numpy as jnp
from jax import lax
from jax.sharding import PartitionSpec as P


def local(inputs, out_grad, kernel, gate_weight, right_factor, left_factor):
    block = right_factor.shape[0]
    rows, width = inputs.shape
    model_width = gate_weight.shape[0]
    local_blocks = rows // block
    blocks_in = inputs.reshape(local_blocks, block, width)
    first = jnp.einsum(
        "abc,jb->ajc", blocks_in, right_factor, preferred_element_type=jnp.float32
    ).astype(jnp.bfloat16)
    scaled = (first.astype(jnp.float32) * kernel.astype(jnp.float32)).astype(jnp.bfloat16)
    piece = lax.all_to_all(scaled, "seq", split_axis=1, concat_axis=0, tiled=True)
    product = jnp.einsum("ia,ajc->jic", left_factor, piece, preferred_element_type=jnp.float32)
    mixed_cube = product.astype(jnp.bfloat16)
    mixed = mixed_cube.reshape(rows, width)
    full_weight = lax.all_gather(gate_weight, "chan", axis=1, tiled=True)
    rows_in = lax.all_to_all(inputs, "chan", split_axis=0, concat_axis=1, tiled=True)
    pre_tok = jnp.dot(rows_in, full_weight, preferred_element_type=jnp.float32)
    gate_tok = jax.nn.sigmoid(pre_tok).astype(jnp.bfloat16)
    gate = lax.all_to_all(gate_tok, "chan", split_axis=1, concat_axis=0, tiled=True)
    gate_wide = gate.astype(jnp.float32)
    cot_wide = out_grad.astype(jnp.float32)
    grad_mixed = (cot_wide * gate_wide).astype(jnp.bfloat16)
    grad_pre = (cot_wide * mixed.astype(jnp.float32) * gate_wide * (1.0 - gate_wide)).astype(
        jnp.bfloat16
    )
    pre_rows = lax.all_to_all(grad_pre, "chan", split_axis=0, concat_axis=1, tiled=True)
    gate_in_rows = jnp.einsum(
        "nk,dk->nd", pre_rows, full_weight, preferred_element_type=jnp.float32
    ).astype(jnp.bfloat16)
    weight_raw = jnp.einsum("nd,nk->dk", rows_in, pre_rows, preferred_element_type=jnp.float32)
    gate_input_grad = lax.all_to_all(gate_in_rows, "chan", split_axis=1, concat_axis=0, tiled=True)
    grad_cube = grad_mixed.reshape(local_blocks, block, width)
    grad_mid = jnp.einsum(
        "ia,jic->ajc", left_factor, grad_cube, preferred_element_type=jnp.float32
    ).astype(jnp.bfloat16)
    left_raw = jnp.einsum("jic,ajc->ia", grad_cube, piece, preferred_element_type=jnp.float32)
    grad_blocks = lax.all_to_all(grad_mid, "seq", split_axis=0, concat_axis=1, tiled=True)
    grad_wide = grad_blocks.astype(jnp.float32)
    grad_first = (grad_wide * kernel.astype(jnp.float32)).astype(jnp.bfloat16)
    kernel_grad = (grad_wide * first.astype(jnp.float32)).astype(jnp.bfloat16)
    right_raw = jnp.einsum("ajc,abc->jb", grad_first, blocks_in, preferred_element_type=jnp.float32)
    back = jnp.einsum(
        "ajc,jb->abc", grad_first, right_factor, preferred_element_type=jnp.float32
    ).reshape(rows, width)
    input_grad = (back + gate_input_grad.astype(jnp.float32)).astype(jnp.bfloat16)
    right_flat = right_raw.reshape(block * block)
    left_flat = left_raw.reshape(block * block)
    right_share, left_share, weight_share = (
        lax.psum_scatter(right_flat, ("seq", "chan"), scatter_dimension=0, tiled=True),
        lax.psum_scatter(left_flat, ("seq", "chan"), scatter_dimension=0, tiled=True),
        lax.psum_scatter(weight_raw, ("seq", "chan"), scatter_dimension=0, tiled=True),
    )
    factor_scale = 1.0 / jnp.sqrt(jnp.float32(block * model_width))
    token_scale = 1.0 / jnp.sqrt(jnp.float32(block * block))
    return (
        input_grad,
        kernel_grad,
        right_share * factor_scale,
        left_share * factor_scale,
        weight_share * token_scale,
    )


def solution(mesh):
    in_specs = (
        P("seq", "chan"),
        P("seq", "chan"),
        P("seq", None, "chan"),
        P(None, "chan"),
        P(),
        P(),
    )
    out_specs = (
        P("seq", "chan"),
        P("seq", None, "chan"),
        P(("seq", "chan")),
        P(("seq", "chan")),
        P(("seq", "chan"), None),
    )
    return jax.shard_map(local, mesh=mesh, in_specs=in_specs, out_specs=out_specs, check_vma=False)
```

profile of v0, /device:TPU:2, one launch (start us, length us, event | category | flops | bytes accessed | tf_op | source)
XLA Modules:
  0.0 548.6 jit_solution(11313670629219693192)
XLA Ops:
  7.2 0.0 copy-start
  7.2 0.0 copy-start.1
  7.2 6.2 %all-to-all-start = ((bf16[8,1024,128]{2,1,0:T(8,128)(2,1)}), bf16[8,1024,128]{2,1,0:T(8,128)(2,1)}, u32[]{:S(2)}, u32[]{:S(2)}) async-start(bf16[8,1024,128]{2,1,0:T(8,128)(2,1)} %bitcast.87), calls=%async_computation | async-start | bytes 4194304 | tf_op jit(solution)/shard_map/all_to_all | solution.py:22
  13.4 0.0 all-gather.2.cloned.1.call-start
  13.4 0.7 all-gather.2.cloned.1.call-update
  14.1 0.0 copy-done
  14.1 0.0 copy-done.1
  14.1 4.2 fusion.5
  18.3 2.6 copy.67
  21.0 21.7 %all-to-all-done = bf16[8,1024,128]{2,1,0:T(8,128)(2,1)} async-done(((bf16[8,1024,128]{2,1,0:T(8,128)(2,1)}), bf16[8,1024,128]{2,1,0:T(8,128)(2,1)}, u32[]{:S(2)}, u32[]{:S(2)}) %all-to-all-start) | async-done | bytes 2097184 | tf_op jit(solution)/shard_map/all_to_all | solution.py:22
  42.7 10.1 %all-to-all-start.3 = ((bf16[16,512,128]{2,0,1:T(8,128)(2,1)}), bf16[16,512,128]{2,0,1:T(8,128)(2,1)}, u32[]{:S(2)}, u32[]{:S(2)}) async-start(bf16[16,512,128]{2,0,1:T(8,128)(2,1)} %copy.67), calls=%async_computation.3 | async-start | bytes 4194304 | tf_op jit(solution)/shard_map/all_to_all | solution.py:17
  52.8 3.9 copy.60
  56.8 35.6 %all-gather.2.cloned.1.call-done = bf16[1024,1024]{1,0:T(8,128)(2,1)} async-done(((bf16[1024,128]{1,0:T(8,128)(2,1)}), bf16[1024,1024]{1,0:T(8,128)(2,1)}) %all-gather.2.cloned.1.call-update) | async-done | bytes 2097168 | tf_op jit(solution)/shard_map/all_gather | solution.py:21
  92.4 6.5 %divide_convert_fusion = bf16[1024,1024]{0,1:T(8,128)(2,1)} fusion(bf16[1024,1024]{0,1:T(8,128)(2,1)} %bitcast.97, bf16[1024,1024]{1,0:T(8,128)(2,1)} %all-gather.2.cloned.1.call-done), kind=kOutput, calls=%fused_computation.19 | convolution fusion | flops 2151677952 | bytes 6291456 | tf_op jit(solution)/shard_map/dot_general | solution.py:23
  98.9 3.0 all-to-all-done.3
  101.9 4.4 all-to-all-start.1
  106.3 0.0 copy-start.7
  106.3 2.2 copy.69
  108.5 0.0 copy-start.4
  108.5 1.3 copy-done.4
  109.9 0.0 copy-done.7
  109.9 3.4 convert_bitcast_fusion.2
  113.2 5.3 copy.71
  118.5 14.5 %all-to-all-done.1 = bf16[1024,8,128]{0,2,1:T(8,128)(2,1)} async-done(((bf16[1024,8,128]{0,2,1:T(8,128)(2,1)}), bf16[1024,8,128]{0,2,1:T(8,128)(2,1)}, u32[]{:S(2)}, u32[]{:S(2)}) %all-to-all-start.1) | async-done | bytes 2097184 | tf_op jit(solution)/shard_map/all_to_all | solution.py:25
  133.1 4.1 convert_bitcast_fusion.3
  137.1 5.4 copy.61
  142.5 7.2 %fusion = (bf16[8192,128]{1,0:T(8,128)(2,1)}, bf16[8192,128]{1,0:T(8,128)(2,1)}) fusion(bf16[8192,128]{1,0:T(8,128)(2,1)} %param.7, f32[8,1024,128]{2,1,0:T(8,128)} %copy.61, f32[16,512,128]{2,1,0:T(8,128)} %copy.71), kind=kLoop, calls=%fused_computation.4 | loop fusion | flops 8388608 | bytes 14680064 | tf_op jit(solution)/shard_map/convert_element_type | solution.py:28
  149.7 4.0 copy.72
  153.7 4.7 all-to-all-start.4
  158.5 4.2 convert_bitcast_fusion.4
  162.7 4.6 copy.63
  167.3 17.9 %all-to-all-done.4 = bf16[8,1024,128]{1,2,0:T(8,128)(2,1)} async-done(((bf16[8,1024,128]{1,2,0:T(8,128)(2,1)}), bf16[8,1024,128]{1,2,0:T(8,128)(2,1)}, u32[]{:S(2)}, u32[]{:S(2)}) %all-to-all-start.4) | async-done | bytes 2097184 | tf_op jit(solution)/shard_map/all_to_all | solution.py:32
  185.2 6.1 %all-to-all-start.2 = ((bf16[512,16,128]{2,1,0:T(8,128)(2,1)}), bf16[512,16,128]{2,1,0:T(8,128)(2,1)}, u32[]{:S(2)}, u32[]{:S(2)}) async-start(bf16[512,16,128]{2,1,0:T(8,128)(2,1)} %copy.63), calls=%async_computation.2 | async-start | bytes 4194304 | tf_op jit(solution)/shard_map/all_to_all | solution.py:43
  191.3 3.5 fusion.11
  194.8 0.0 copy-start.8
  194.8 1.3 copy.82
  196.1 0.7 copy-done.8
  196.8 5.3 convolution_convert_fusion
  202.0 38.3 %all-to-all-done.2 = bf16[512,16,128]{2,1,0:T(8,128)(2,1)} async-done(((bf16[512,16,128]{2,1,0:T(8,128)(2,1)}), bf16[512,16,128]{2,1,0:T(8,128)(2,1)}, u32[]{:S(2)}, u32[]{:S(2)}) %all-to-all-start.2) | async-done | bytes 2097184 | tf_op jit(solution)/shard_map/all_to_all | solution.py:43
  240.3 4.8 all-to-all-start.5
  245.1 0.0 all-reduce.6.cloned.1.call-start
  245.2 6.5 %convolution_bitcast_fusion = f32[1024,1024]{0,1:T(8,128)} fusion(bf16[1024,1024]{0,1:T(8,128)(2,1)} %bitcast.25, bf16[1024,1024]{0,1:T(8,128)(2,1)} %bitcast.98), kind=kOutput, calls=%fused_computation.20 | convolution fusion | flops 2147483648 | bytes 8388608 | tf_op jit(solution)/shard_map/nd,nk->dk/dot_general | solution.py:36
  251.7 2.1 convert_bitcast_fusion
  253.8 0.0 copy-start.2
  253.8 0.0 copy-start.3
  253.8 0.4 copy.64
  254.3 1.1 copy-done.2
  255.4 0.6 copy-done.3
  256.0 2.6 fusion.7
  258.6 1.3 convolution_bitcast_fusion.2
  259.9 0.0 copy-done.5
  259.9 1.3 copy.81
  261.3 0.0 all-reduce.6.cloned.1.call-update
  261.3 10.4 %all-to-all-done.5 = bf16[1024,8,128]{0,2,1:T(8,128)(2,1)} async-done(((bf16[1024,8,128]{0,2,1:T(8,128)(2,1)}), bf16[1024,8,128]{0,2,1:T(8,128)(2,1)}, u32[]{:S(2)}, u32[]{:S(2)}) %all-to-all-start.5) | async-done | bytes 2097184 | tf_op jit(solution)/shard_map/all_to_all | solution.py:37
  271.7 4.3 convert_bitcast_fusion.1
  276.0 5.5 %copy.73 = f32[8,1024,128]{2,1,0:T(8,128)} copy(f32[8,1024,128]{1,2,0:T(8,128)} %convert_bitcast_fusion.1) | data formatting | bytes 8388608 | tf_op jit(solution)/shard_map/convert_element_type | solution.py:51
  281.5 0.0 copy-done.6
  281.5 3.2 convolution_bitcast_fusion.1
  284.7 5.4 copy.66
  290.1 5.3 fusion.6
  295.4 243.0 %all-reduce.6.cloned.1.call-done = (f32[262144]{0:T(1024)}, f32[262144]{0:T(1024)}, f32[1024,1024]{0,1:T(8,128)}) async-done(((f32[262144]{0:T(1024)}, f32[262144]{0:T(1024)}, f32[1024,1024]{0,1:T(8,128)}), (f32[262144]{0:T(1024)}, f32[262144]{0:T(1024)}, f32[1024,1024]{0,1:T(8,128)})) %all-reduce.6.cloned.1.call-update) | async-done | bytes 6291472
  538.4 1.2 dynamic-slice_multiply_fusion
  539.6 0.8 copy.75
  540.4 1.3 dynamic-slice_multiply_fusion.1
  (2 shorter events, 0.0 us)
Async XLA Ops:
  7.2 6.9 %copy-start = (bf16[512,512]{1,0:T(8,128)(2,1)S(1)}, bf16[512,512]{1,0:T(8,128)(2,1)}, u32[]{:S(2)}) copy-start(bf16[512,512]{1,0:T(8,128)(2,1)} %param.10) | copy-start | bytes 1572868
  7.2 6.9 %copy-start.1 = (bf16[8192,128]{1,0:T(8,128)(2,1)S(1)}, bf16[8192,128]{1,0:T(8,128)(2,1)}, u32[]{:S(2)}) copy-start(bf16[8192,128]{1,0:T(8,128)(2,1)} %param.6) | copy-start | bytes 6291460
  7.2 35.5 %all-to-all-start = ((bf16[8,1024,128]{2,1,0:T(8,128)(2,1)}), bf16[8,1024,128]{2,1,0:T(8,128)(2,1)}, u32[]{:S(2)}, u32[]{:S(2)}) async-start(bf16[8,1024,128]{2,1,0:T(8,128)(2,1)} %bitcast.87), calls=%async_computation | async-start | bytes 4194304 | tf_op jit(solution)/shard_map/all_to_all | solution.py:22
  13.4 79.0 %all-gather.2.cloned.1.call-start = ((), (), s32[]{:S(2)}) async-start(), calls=%async_computation.6 | async-start | bytes 2359296 | tf_op jit(solution)/shard_map/all_gather | solution.py:21
  42.7 59.2 %all-to-all-start.3 = ((bf16[16,512,128]{2,0,1:T(8,128)(2,1)}), bf16[16,512,128]{2,0,1:T(8,128)(2,1)}, u32[]{:S(2)}, u32[]{:S(2)}) async-start(bf16[16,512,128]{2,0,1:T(8,128)(2,1)} %copy.67), calls=%async_computation.3 | async-start | bytes 4194304 | tf_op jit(solution)/shard_map/all_to_all | solution.py:17
  101.9 31.1 %all-to-all-start.1 = ((bf16[1024,8,128]{0,2,1:T(8,128)(2,1)}), bf16[1024,8,128]{0,2,1:T(8,128)(2,1)}, u32[]{:S(2)}, u32[]{:S(2)}) async-start(bf16[1024,8,128]{0,2,1:T(8,128)(2,1)} %bitcast.100), calls=%async_computation.1 | async-start | bytes 4194304 | tf_op jit(solution)/shard_map/all_to_all | solution.py:25
  106.3 3.6 copy-start.7
  108.5 1.4 copy-start.4
  153.7 31.4 %all-to-all-start.4 = ((bf16[8,1024,128]{1,2,0:T(8,128)(2,1)}), bf16[8,1024,128]{1,2,0:T(8,128)(2,1)}, u32[]{:S(2)}, u32[]{:S(2)}) async-start(bf16[8,1024,128]{1,2,0:T(8,128)(2,1)} %copy.72), calls=%async_computation.4 | async-start | bytes 4194304 | tf_op jit(solution)/shard_map/all_to_all | solution.py:32
  185.2 55.2 %all-to-all-start.2 = ((bf16[512,16,128]{2,1,0:T(8,128)(2,1)}), bf16[512,16,128]{2,1,0:T(8,128)(2,1)}, u32[]{:S(2)}, u32[]{:S(2)}) async-start(bf16[512,16,128]{2,1,0:T(8,128)(2,1)} %copy.63), calls=%async_computation.2 | async-start | bytes 4194304 | tf_op jit(solution)/shard_map/all_to_all | solution.py:43
  194.8 2.0 copy-start.8
  240.3 31.3 %all-to-all-start.5 = ((bf16[1024,8,128]{0,2,1:T(8,128)(2,1)}), bf16[1024,8,128]{0,2,1:T(8,128)(2,1)}, u32[]{:S(2)}, u32[]{:S(2)}) async-start(bf16[1024,8,128]{0,2,1:T(8,128)(2,1)} %bitcast.99), calls=%async_computation.5 | async-start | bytes 4194304 | tf_op jit(solution)/shard_map/all_to_all | solution.py:37
  245.1 293.3 %all-reduce.6.cloned.1.call-start = ((), (), s32[]{:S(2)}) async-start(), calls=%async_computation.7 | async-start | bytes 12582912
  253.8 1.6 copy-start.2
  253.8 2.2 copy-start.3
  258.6 1.3 copy-start.5
  276.0 5.5 %copy-start.6 = (bf16[16,512,128]{2,1,0:T(8,128)(2,1)S(1)}, bf16[16,512,128]{2,1,0:T(8,128)(2,1)}, u32[]{:S(2)}) copy-start(bf16[16,512,128]{2,1,0:T(8,128)(2,1)} %copy-done.5) | copy-start | bytes 6291460
Sparse Core Ops, SparseCore 0:
  16.6 75.7 all-gather.1
  261.4 276.9 all-reduce.5
where the time goes:
time: 550 us; the launch traced here: 549 us
  waiting for transfers between devices  385 us (70%)
  local copies, waits for them, and re-layouts  46.7 us (8%)
  matrix products  38.1 us (7%)
  starting transfers between devices  36.4 us (7%)
  other arithmetic  28.1 us (5%)
  between operations  14.2 us (3%)
    unnamed x3, waiting for transfers between devices  244 us
    all_to_all x1, waiting for transfers between devices, local(): lax.all_to_all(grad_mid, 'seq', split_axis=0, concat_axis=1, tiled=True)  38.3 us
    all_gather x1, waiting for transfers between devices, local(): full_weight = lax.all_gather(gate_weight, 'chan', axis=1, tiled=True)  35.6 us
    all_to_all x1, waiting for transfers between devices, local(): lax.all_to_all(inputs, 'chan', split_axis=0, concat_axis=1, tiled=True)  21.7 us
    all_to_all x1, waiting for transfers between devices, local(): lax.all_to_all(grad_pre, 'chan', split_axis=0, concat_axis=1, tiled=True)  17.9 us
    all_to_all x1, waiting for transfers between devices, local(): lax.all_to_all(gate_tok, 'chan', split_axis=1, concat_axis=0, tiled=True)  14.5 us
  transfers between devices with their start and end apart: 8, of which 8 were waited for; matrix products, arithmetic and copies ran while one was open for 16% of the time, Pallas kernels for 0%

commit v1 on v0

--- a/solution.py
+++ b/solution.py
@@ -2,6 +2,16 @@
 import jax.numpy as jnp
 from jax import lax
 from jax.sharding import PartitionSpec as P
+
+ranges_raise = lambda arr, where_dim: jnp.concatenate(
+    jax.lax.all_to_all(
+        jnp.stack([arr for _ in range(jax.lax.axis_size("chan"))], axis=0),
+        split_axis=0,
+        concat_axis=0,
+        axis_name="chan",
+    ),
+    axis=where_dim,
+)
 
 
 def local(inputs, out_grad, kernel, gate_weight, right_factor, left_factor):
@@ -18,7 +28,7 @@
     product = jnp.einsum("ia,ajc->jic", left_factor, piece, preferred_element_type=jnp.float32)
     mixed_cube = product.astype(jnp.bfloat16)
     mixed = mixed_cube.reshape(rows, width)
-    full_weight = lax.all_gather(gate_weight, "chan", axis=1, tiled=True)
+    full_weight = ranges_raise(gate_weight, 1)
     rows_in = lax.all_to_all(inputs, "chan", split_axis=0, concat_axis=1, tiled=True)
     pre_tok = jnp.dot(rows_in, full_weight, preferred_element_type=jnp.float32)
     gate_tok = jax.nn.sigmoid(pre_tok).astype(jnp.bfloat16)

time: 550 us -> 589 us (1.071)
  blocking collectives: 0 us -> 34.5 us
    all_to_all x1, waiting for transfers between devices: 3.05 us -> 39.7 us  [local(): lax.all_to_all(scaled, 'seq', split_axis=1, concat_axis=0, tiled=True)]
    all_gather x1 -> x0, waiting for transfers between devices: 35.6 us -> none  [local(): full_weight = lax.all_gather(gate_weight, 'chan', axis=1, tiled=True)]
    all_to_all x0 -> x1, blocking collectives: none -> 34.5 us  [jax.lax.all_to_all(jnp.stack([arr for _ in range(jax.lax.axis_size('chan'...]
    unnamed x3 -> x2, waiting for transfers between devices: 244 us -> 245 us
  transfers between devices with their start and end apart: 8 -> 7, of which waited for: 8 -> 7; matrix products, arithmetic and copies ran while one was open for 16% -> 14% of each run, Pallas kernels for 0% -> 0%
where the time goes in v1:
time: 589 us; the launch traced here: 588 us
  waiting for transfers between devices  388 us (66%)
  local copies, waits for them, and re-layouts  47.9 us (8%)
  matrix products  41 us (7%)
  starting transfers between devices  35.1 us (6%)
  blocking collectives  34.5 us (6%)
  other arithmetic  27.7 us (5%)
  between operations  14.2 us (2%)
    unnamed x2, waiting for transfers between devices  245 us
    all_to_all x1, waiting for transfers between devices, local(): lax.all_to_all(scaled, 'seq', split_axis=1, concat_axis=0, tiled=True)  39.7 us
    all_to_all x1, blocking collectives, jax.lax.all_to_all(jnp.stack([arr for _ in range(jax.lax.axis_size('chan'...  34.5 us
    all_to_all x1, waiting for transfers between devices, local(): lax.all_to_all(grad_mid, 'seq', split_axis=0, concat_axis=1, tiled=True)  34.4 us
    all_to_all x1, waiting for transfers between devices, local(): lax.all_to_all(inputs, 'chan', split_axis=0, concat_axis=1, tiled=True)  22.3 us
    all_to_all x1, waiting for transfers between devices, local(): lax.all_to_all(gate_tok, 'chan', split_axis=1, concat_axis=0, tiled=True)  19.8 us
    all_to_all x1, waiting for transfers between devices, local(): lax.all_to_all(grad_pre, 'chan', split_axis=0, concat_axis=1, tiled=True)  17.9 us
  transfers between devices with their start and end apart: 7, of which 7 were waited for; matrix products, arithmetic and copies ran while one was open for 14% of the time, Pallas kernels for 0%

profile of v1, /device:TPU:2, one launch (start us, length us, event | category | flops | bytes accessed | tf_op | source)
XLA Modules:
  0.0 588.1 jit_solution(3062601353593710709)
XLA Ops:
  7.2 0.0 copy-start
  7.2 1.3 stack.2
  8.5 34.5 %all_to_all.96 = bf16[8,1024,128]{2,1,0:T(8,128)(2,1)S(1)} all-to-all(bf16[8,1024,128]{2,1,0:T(8,128)(2,1)S(1)} %stack.2), channel_id=1, replica_groups=mesh['seq'=32,'chan'=8] {'chan'}, dimensions={0} | all-to-all | bytes 4194304 | tf_op jit(solution)/shard_map/all_to_all | solution.py:7
  42.9 0.0 copy-start.3
  42.9 4.3 all-to-all-start
  47.3 0.0 copy-done.3
  47.3 2.6 copy.64
  49.9 22.3 %all-to-all-done = bf16[8,1024,128]{2,1,0:T(8,128)(2,1)} async-done(((bf16[8,1024,128]{2,1,0:T(8,128)(2,1)}), bf16[8,1024,128]{2,1,0:T(8,128)(2,1)}, u32[]{:S(2)}, u32[]{:S(2)}) %all-to-all-start) | async-done | bytes 2097184 | tf_op jit(solution)/shard_map/all_to_all | solution.py:32
  72.2 2.9 copy.63
  75.0 0.0 copy-start.7
  75.0 6.4 %divide_convert_fusion = bf16[1024,1024]{0,1:T(8,128)(2,1)} fusion(bf16[1024,1024]{0,1:T(8,128)(2,1)} %bitcast.105, bf16[1024,1024]{0,1:T(8,128)(2,1)S(1)} %bitcast.100), kind=kOutput, calls=%fused_computation.20 | convolution fusion | flops 2151677952 | bytes 6291456 | tf_op jit(solution)/shard_map/dot_general | solution.py:33
  81.4 0.0 copy-done.7
  81.4 0.0 copy-start.1
  81.4 4.9 all-to-all-start.2
  86.3 0.0 copy-done
  86.3 0.0 copy-done.1
  86.4 4.2 fusion.5
  90.6 2.7 copy.71
  93.2 19.8 %all-to-all-done.2 = bf16[1024,8,128]{0,2,1:T(8,128)(2,1)} async-done(((bf16[1024,8,128]{0,2,1:T(8,128)(2,1)}), bf16[1024,8,128]{0,2,1:T(8,128)(2,1)}, u32[]{:S(2)}, u32[]{:S(2)}) %all-to-all-start.2) | async-done | bytes 2097184 | tf_op jit(solution)/shard_map/all_to_all | solution.py:35
  113.0 10.1 %all-to-all-start.4 = ((bf16[16,512,128]{2,0,1:T(8,128)(2,1)}), bf16[16,512,128]{2,0,1:T(8,128)(2,1)}, u32[]{:S(2)}, u32[]{:S(2)}) async-start(bf16[16,512,128]{2,0,1:T(8,128)(2,1)} %copy.71), calls=%async_computation.4 | async-start | bytes 4194304 | tf_op jit(solution)/shard_map/all_to_all | solution.py:27
  123.2 4.1 convert_bitcast_fusion.3
  127.3 5.3 copy.65
  132.6 39.7 %all-to-all-done.4 = bf16[16,512,128]{2,0,1:T(8,128)(2,1)} async-done(((bf16[16,512,128]{2,0,1:T(8,128)(2,1)}), bf16[16,512,128]{2,0,1:T(8,128)(2,1)}, u32[]{:S(2)}, u32[]{:S(2)}) %all-to-all-start.4) | async-done | bytes 2097184 | tf_op jit(solution)/shard_map/all_to_all | solution.py:27
  172.3 0.0 copy-start.8
  172.3 2.2 copy.73
  174.5 0.0 copy-start.4
  174.5 1.3 copy-done.4
  175.8 0.0 copy-done.8
  175.8 3.3 convert_bitcast_fusion.2
  179.1 5.4 copy.75
  184.5 7.2 %fusion = (bf16[8192,128]{1,0:T(8,128)(2,1)}, bf16[8192,128]{1,0:T(8,128)(2,1)}) fusion(bf16[8192,128]{1,0:T(8,128)(2,1)} %param.7, f32[8,1024,128]{2,1,0:T(8,128)} %copy.65, f32[16,512,128]{2,1,0:T(8,128)} %copy.75), kind=kLoop, calls=%fused_computation.4 | loop fusion | flops 8388608 | bytes 14680064 | tf_op jit(solution)/shard_map/convert_element_type | solution.py:38
  191.8 4.8 all-to-all-start.5
  196.5 4.2 convert_bitcast_fusion.4
  200.7 4.5 copy.67
  205.2 17.9 %all-to-all-done.5 = bf16[8,1024,128]{2,1,0:T(8,128)(2,1)} async-done(((bf16[8,1024,128]{2,1,0:T(8,128)(2,1)}), bf16[8,1024,128]{2,1,0:T(8,128)(2,1)}, u32[]{:S(2)}, u32[]{:S(2)}) %all-to-all-start.5) | async-done | bytes 2097184 | tf_op jit(solution)/shard_map/all_to_all | solution.py:42
  223.1 6.2 %all-to-all-start.3 = ((bf16[512,16,128]{2,1,0:T(8,128)(2,1)}), bf16[512,16,128]{2,1,0:T(8,128)(2,1)}, u32[]{:S(2)}, u32[]{:S(2)}) async-start(bf16[512,16,128]{2,1,0:T(8,128)(2,1)} %copy.67), calls=%async_computation.3 | async-start | bytes 4194304 | tf_op jit(solution)/shard_map/all_to_all | solution.py:53
  229.3 3.5 fusion.11
  232.8 1.3 copy.86
  234.1 3.9 copy.78
  238.0 6.0 %bitcast_convert_fusion = bf16[1024,1024]{0,1:T(8,128)(2,1)} fusion(bf16[8,1024,128]{2,1,0:T(8,128)(2,1)} %all-to-all-done.5, bf16[8,1024,128]{2,1,0:T(8,128)(2,1)} %copy-done.3), kind=kOutput, calls=%fused_computation.13 | convolution fusion | flops 2148532224 | bytes 6291456 | tf_op jit(solution)/shard_map/nk,dk->nd/dot_general | solution.py:43
  244.0 34.4 %all-to-all-done.3 = bf16[512,16,128]{2,1,0:T(8,128)(2,1)} async-done(((bf16[512,16,128]{2,1,0:T(8,128)(2,1)}), bf16[512,16,128]{2,1,0:T(8,128)(2,1)}, u32[]{:S(2)}, u32[]{:S(2)}) %all-to-all-start.3) | async-done | bytes 2097184 | tf_op jit(solution)/shard_map/all_to_all | solution.py:53
  278.4 4.7 all-to-all-start.6
  283.0 0.0 all-reduce.6.cloned.1.call-start
  283.1 6.5 %convolution_bitcast_fusion = f32[1024,1024]{0,1:T(8,128)} fusion(bf16[1024,1024]{0,1:T(8,128)(2,1)} %bitcast.103, bf16[1024,1024]{0,1:T(8,128)(2,1)} %bitcast.101), kind=kOutput, calls=%fused_computation.21 | convolution fusion | flops 2147483648 | bytes 8388608 | tf_op jit(solution)/shard_map/nd,nk->dk/dot_general | solution.py:46
  289.6 2.1 convert_bitcast_fusion
  291.7 0.0 copy-start.2
  291.7 0.4 copy.68
  292.2 1.1 copy-done.2
  293.3 2.5 fusion.7
  295.8 3.6 convolution_bitcast_fusion.2
  299.4 0.0 copy-done.5
  299.5 1.3 copy.85
  300.8 0.0 all-reduce.6.cloned.1.call-update
  300.8 8.8 %all-to-all-done.6 = bf16[1024,8,128]{0,2,1:T(8,128)(2,1)} async-done(((bf16[1024,8,128]{0,2,1:T(8,128)(2,1)}), bf16[1024,8,128]{0,2,1:T(8,128)(2,1)}, u32[]{:S(2)}, u32[]{:S(2)}) %all-to-all-start.6) | async-done | bytes 2097184 | tf_op jit(solution)/shard_map/all_to_all | solution.py:47
  309.6 4.0 convert_bitcast_fusion.1
  313.6 5.5 copy.76
  319.1 0.0 copy-done.6
  319.1 3.2 convolution_bitcast_fusion.1
  322.3 5.4 copy.70
  327.7 5.3 fusion.6
  333.0 244.9 %all-reduce.6.cloned.1.call-done = (f32[262144]{0:T(1024)}, f32[262144]{0:T(1024)}, f32[1024,1024]{0,1:T(8,128)}) async-done(((f32[262144]{0:T(1024)}, f32[262144]{0:T(1024)}, f32[1024,1024]{0,1:T(8,128)}), (f32[262144]{0:T(1024)}, f32[262144]{0:T(1024)}, f32[1024,1024]{0,1:T(8,128)})) %all-reduce.6.cloned.1.call-update) | async-done | bytes 6291472
  577.9 1.2 dynamic-slice_multiply_fusion
  579.1 0.8 copy.79
  579.9 1.3 dynamic-slice_multiply_fusion.1
  (2 shorter events, 0.0 us)
Async XLA Ops:
  7.2 79.2 %copy-start = (bf16[512,512]{1,0:T(8,128)(2,1)S(1)}, bf16[512,512]{1,0:T(8,128)(2,1)}, u32[]{:S(2)}) copy-start(bf16[512,512]{1,0:T(8,128)(2,1)} %param.10) | copy-start | bytes 1572868
  42.9 4.4 copy-start.3
  42.9 29.2 %all-to-all-start = ((bf16[8,1024,128]{2,1,0:T(8,128)(2,1)}), bf16[8,1024,128]{2,1,0:T(8,128)(2,1)}, u32[]{:S(2)}, u32[]{:S(2)}) async-start(bf16[8,1024,128]{2,1,0:T(8,128)(2,1)} %bitcast), calls=%async_computation | async-start | bytes 4194304 | tf_op jit(solution)/shard_map/all_to_all | solution.py:32
  75.0 6.4 %copy-start.7 = (bf16[1024,8,128]{0,2,1:T(8,128)(2,1)}, bf16[1024,8,128]{0,2,1:T(8,128)(2,1)S(1)}, u32[]{:S(2)}) copy-start(bf16[1024,8,128]{0,2,1:T(8,128)(2,1)S(1)} %copy.63) | copy-start | bytes 6291460
  81.4 4.9 copy-start.1
  81.4 31.6 %all-to-all-start.2 = ((bf16[1024,8,128]{0,2,1:T(8,128)(2,1)}), bf16[1024,8,128]{0,2,1:T(8,128)(2,1)}, u32[]{:S(2)}, u32[]{:S(2)}) async-start(bf16[1024,8,128]{0,2,1:T(8,128)(2,1)} %bitcast.104), calls=%async_computation.2 | async-start | bytes 4194304 | tf_op jit(solution)/shard_map/all_to_all | solution.py:35
  113.0 59.3 %all-to-all-start.4 = ((bf16[16,512,128]{2,0,1:T(8,128)(2,1)}), bf16[16,512,128]{2,0,1:T(8,128)(2,1)}, u32[]{:S(2)}, u32[]{:S(2)}) async-start(bf16[16,512,128]{2,0,1:T(8,128)(2,1)} %copy.71), calls=%async_computation.4 | async-start | bytes 4194304 | tf_op jit(solution)/shard_map/all_to_all | solution.py:27
  172.3 3.5 copy-start.8
  174.5 1.3 copy-start.4
  191.8 31.3 %all-to-all-start.5 = ((bf16[8,1024,128]{2,1,0:T(8,128)(2,1)}), bf16[8,1024,128]{2,1,0:T(8,128)(2,1)}, u32[]{:S(2)}, u32[]{:S(2)}) async-start(bf16[8,1024,128]{2,1,0:T(8,128)(2,1)} %bitcast.94), calls=%async_computation.5 | async-start | bytes 4194304 | tf_op jit(solution)/shard_map/all_to_all | solution.py:42
  223.1 55.3 %all-to-all-start.3 = ((bf16[512,16,128]{2,1,0:T(8,128)(2,1)}), bf16[512,16,128]{2,1,0:T(8,128)(2,1)}, u32[]{:S(2)}, u32[]{:S(2)}) async-start(bf16[512,16,128]{2,1,0:T(8,128)(2,1)} %copy.67), calls=%async_computation.3 | async-start | bytes 4194304 | tf_op jit(solution)/shard_map/all_to_all | solution.py:53
  278.4 31.2 %all-to-all-start.6 = ((bf16[1024,8,128]{0,2,1:T(8,128)(2,1)}), bf16[1024,8,128]{0,2,1:T(8,128)(2,1)}, u32[]{:S(2)}, u32[]{:S(2)}) async-start(bf16[1024,8,128]{0,2,1:T(8,128)(2,1)} %bitcast.102), calls=%async_computation.6 | async-start | bytes 4194304 | tf_op jit(solution)/shard_map/all_to_all | solution.py:47
  283.0 294.8 %all-reduce.6.cloned.1.call-start = ((), (), s32[]{:S(2)}) async-start(), calls=%async_computation.7 | async-start | bytes 12582912
  291.7 1.6 copy-start.2
  295.8 3.6 copy-start.5
  313.6 5.5 copy-start.6
Sparse Core Ops, SparseCore 0:
  300.9 276.8 all-reduce.5
